TPU v7x, 32 devices: a whole 2x2x4 slice. The times are simulated.
32 devices in a mesh: chan: 4 (over y, x), space: 4 (over z), rep: 2 (over core).
Axes of the slice: x: 2, y: 2, z: 4, core: 2. Of those that a mesh axis runs over, the one named last changes fastest.
Arguments:
- inputs: bfloat16 [2, 2, 16, 512, 128], P('rep', None, 'space', 'chan'), may hold values from -6 to 6
- grad_out: bfloat16 [2, 2, 16, 512, 128], P('rep', None, 'space', 'chan'), may hold values from -6 to 6
- weight: bfloat16 [3, 3, 3, 512, 512], P(None, None, None, 'chan'), may hold values from -0.0546875 to 0.0546875
Outputs:
- grad_in: bfloat16 [2, 2, 16, 512, 128], P('rep', None, 'space', 'chan')
- grad_weight: float32 [3, 3, 3, 512, 512], P(None, None, None, ('chan', 'rep'))
All inputs are finite; a program needn't handle non-finite values.
Results may differ from a plain program's by a relative error of at most 0.0031.
Values may be sent and summed in bfloat16 or wider, within the bound.
A program may use at most 64 MiB of HBM per device.

v0:
```python
import jax
import jax.numpy as jnp
from jax import lax
from jax.sharding import PartitionSpec as P


def with_halo(cells, sides, width):
    for axis, dim in sides:
        count = lax.axis_size(axis)
        ends = count - 1
        head = lax.slice_in_dim(cells, 0, width, axis=dim)
        tail = lax.slice_in_dim(cells, cells.shape[dim] - width, cells.shape[dim], axis=dim)
        cells = jnp.concatenate(
            [
                lax.ppermute(tail, axis, [(i, (i + 1) % count) for i in range(ends)]),
                cells,
                lax.ppermute(head, axis, [((i + 1) % count, i) for i in range(ends)]),
            ],
            axis=dim,
        )
    return cells


def silu_slope(values):
    logistic = jax.nn.sigmoid(values)
    return logistic * (1.0 + values * (1.0 - logistic))


def tap_windows(padded, frame_count, row_count, col_count):
    windows = []
    for frame_tap in range(3):
        for row_tap in range(3):
            for col_tap in range(3):
                windows.append(
                    padded[
                        :,
                        2 - frame_tap : 2 - frame_tap + frame_count,
                        2 - row_tap : 2 - row_tap + row_count,
                        :,
                        2 - col_tap : 2 - col_tap + col_count,
                    ]
                )
    return jnp.concatenate(windows, axis=3)


def on_device(inputs, grad_out, weight):
    clip_count, frame_count, row_count, in_part, col_count = inputs.shape
    out_part = grad_out.shape[3]
    gathered = lax.all_gather(inputs, "chan", axis=3, tiled=True)
    activated = jax.nn.silu(gathered.astype(jnp.float32)).astype(jnp.bfloat16)
    in_width = activated.shape[3]
    grad_rim = with_halo(grad_out, (("space", 2),), 1)
    grad_pad = jnp.pad(grad_rim, ((0, 0), (0, 2), (0, 0), (0, 0), (1, 1)))
    stacked = tap_windows(grad_pad, frame_count, row_count, col_count)
    local_flat = jnp.einsum(
        "cthkw,cthiw->ki", stacked, activated, preferred_element_type=jnp.float32
    )
    local_weight = local_flat.reshape(3, 3, 3, out_part, in_width)
    clip_summed = lax.psum_scatter(local_weight, "rep", scatter_dimension=3, tiled=True)
    summed = lax.psum(clip_summed, "space")
    grad_weight = summed * (1.0 / 256.0)
    flat_kernel = weight.reshape(27 * out_part, weight.shape[4])
    partial_value = jnp.einsum(
        "cthkw,ki->cthiw", stacked, flat_kernel, preferred_element_type=jnp.float32
    )
    active_grad = lax.psum_scatter(partial_value, "chan", scatter_dimension=3, tiled=True)
    grad_in = (active_grad * silu_slope(inputs.astype(jnp.float32))).astype(jnp.bfloat16)
    return (grad_in, grad_weight)


def solution(mesh):
    return jax.shard_map(
        on_device,
        mesh=mesh,
        in_specs=(
            P("rep", None, "space", "chan", None),
            P("rep", None, "space", "chan", None),
            P(None, None, None, "chan", None),
        ),
        out_specs=(
            P("rep", None, "space", "chan", None),
            P(None, None, None, ("chan", "rep"), None),
        ),
        check_vma=False,
    )
```

profile of v0, /device:TPU:0, one launch (start us, length us, event | category | flops | bytes accessed | tf_op | source)
XLA Modules:
  0.0 258.9 jit_solution(6788880601391279087)
XLA Ops:
  7.2 1.9 copy.15
  9.2 1.5 fusion.32
  10.7 1.3 collective-permute-start.1
  12.0 6.2 %collective-permute-start = (bf16[1,2,1,128,128]{3,4,2,1,0:T(8,128)(2,1)}, bf16[1,2,1,128,128]{3,4,2,1,0:T(8,128)(2,1)}, u32[]{:S(2)}, u32[]{:S(2)}) collective-permute-start(bf16[1,2,1,128,128]{3,4,2,1,0:T(8,128)(2,1)} %get-tuple-element.6), channel_id=1, source_target_pairs={{0,2},{2,4},{4,6},{1,3},{3,5},{5,7},{8,10},{10,12},{12,14},{9,11},... | collective-permute-start | bytes 196616 | tf_op jit(solution)/shard_map/ppermute | solution.py:15
  19.1 0.6 collective-permute-done
  19.7 1.2 fusion.20
  20.9 0.1 slice_dynamic-update-slice_fusion.14
  21.3 0.1 slice_dynamic-update-slice_fusion.10
  21.6 0.1 slice_dynamic-update-slice_fusion.8
  22.0 0.9 fusion.31
  23.4 0.9 fusion.30
  24.4 2.9 %copy-done.2 = bf16[1,2,4,3456,128]{3,4,2,1,0:T(8,128)(2,1)} copy-done((bf16[1,2,4,3456,128]{3,4,2,1,0:T(8,128)(2,1)}, bf16[1,2,4,3456,128]{3,4,2,1,0:T(8,128)(2,1)S(1)}, u32[]{:S(2)}) %copy-start.2) | copy-done | bytes 7077912
  27.3 10.2 %copy.22 = bf16[3456,4,2,128]{3,0,2,1:T(8,128)(2,1)} copy(bf16[3456,4,2,128]{0,3,1,2:T(8,128)(2,1)} %bitcast.31) | data formatting | bytes 14155776 | tf_op jit(solution)/shard_map/cthkw,cthiw->ki/dot_general | solution.py:55
  37.5 8.1 %all-gather.2.cloned.1.call-done = bf16[1,2,4,512,128]{4,3,2,1,0:T(8,128)(2,1)} async-done(((bf16[1,2,4,128,128]{4,3,2,1,0:T(8,128)(2,1)}), bf16[1,2,4,512,128]{4,3,2,1,0:T(8,128)(2,1)}) %all-gather.2.cloned.1.call-update) | async-done | bytes 1048592 | tf_op jit(solution)/shard_map/all_gather | solution.py:49
  45.6 6.6 %fusion = f32[3,3,3,128,512,1,1]{4,3,0,1,2,6,5:T(8,128)S(1)} fusion(bf16[3,3,3,128,4,2,128]{6,3,2,1,0,5,4:T(8,128)(2,1)} %bitcast.32, bf16[1,2,4,512,128]{4,3,2,1,0:T(8,128)(2,1)} %all-gather.2.cloned.1.call-done), kind=kOutput, calls=%fused_computation | convolution fusion | flops 3627024384 | bytes 15204352 | tf_op jit(solution)/shard_map/cthkw,cthiw->ki/dot_general | solution.py:55
  52.3 3.7 %copy.38 = f32[3,3,3,128,512,1,1]{4,3,2,1,0,5,6:T(8,128)} copy(f32[3,3,3,128,512,1,1]{4,3,0,1,2,6,5:T(8,128)S(1)} %fusion) | data formatting | bytes 14155776 | tf_op jit(solution)/shard_map/cthkw,cthiw->ki/dot_general | solution.py:55
  56.1 7.5 %fusion.13 = f32[1,2,4,512,128]{3,4,2,1,0:T(8,128)} fusion(bf16[3456,512,1,1]{1,0,3,2:T(8,128)(2,1)S(1)} %bitcast.29, bf16[1,2,4,3456,128]{3,4,2,1,0:T(8,128)(2,1)} %copy-done.2), kind=kOutput, calls=%fused_computation.20 | convolution fusion | flops 3623878656 | bytes 12713984 | tf_op jit(solution)/shard_map/cthkw,ki->cthiw/dot_general | solution.py:63
  63.7 7.9 %reduce-scatter.5.cloned.1.call-done = f32[3,3,3,64,512]{4,3,2,1,0:T(8,128)} async-done(((f32[3,3,3,128,512]{4,3,2,1,0:T(8,128)}), f32[3,3,3,64,512]{4,3,2,1,0:T(8,128)}) %reduce-scatter.5.cloned.1.call-update) | async-done | bytes 3538960 | tf_op jit(solution)/shard_map/reduce_scatter | solution.py:59
  71.7 1.8 copy.21
  73.5 38.5 %reduce-scatter.3.cloned.1.call-done = f32[1,2,4,128,128]{3,4,2,1,0:T(8,128)} async-done(((f32[1,2,4,512,128]{3,4,2,1,0:T(8,128)}), f32[1,2,4,128,128]{3,4,2,1,0:T(8,128)}) %reduce-scatter.3.cloned.1.call-update) | async-done | bytes 524304 | tf_op jit(solution)/shard_map/reduce_scatter | solution.py:66
  111.9 2.0 fusion.29
  113.9 1.8 copy.25
  115.7 132.2 %all-reduce.3.cloned.1.call-done = f32[3,3,3,64,512]{4,3,2,1,0:T(8,128)} async-done(((f32[3,3,3,64,512]{4,3,2,1,0:T(8,128)}), f32[3,3,3,64,512]{4,3,2,1,0:T(8,128)}) %all-reduce.3.cloned.1.call-update) | async-done | bytes 3538960 | tf_op jit(solution)/shard_map/psum | solution.py:60
  248.0 4.4 %broadcast_multiply_fusion = f32[3,3,3,64,512]{4,3,2,1,0:T(8,128)} fusion(f32[3,3,3,64,512]{4,3,2,1,0:T(8,128)} %all-reduce.3.cloned.1.call-done), kind=kLoop, calls=%fused_computation.13 | loop fusion | flops 884736 | bytes 7077888 | tf_op jit(solution)/shard_map/mul | solution.py:61
  (36 shorter events, 2.2 us)
Async XLA Ops:
  7.2 48.9 %copy-start = (bf16[3,3,3,128,512]{4,3,2,1,0:T(8,128)(2,1)S(1)}, bf16[3,3,3,128,512]{4,3,2,1,0:T(8,128)(2,1)}, u32[]{:S(2)}) copy-start(bf16[3,3,3,128,512]{4,3,2,1,0:T(8,128)(2,1)} %param.5) | copy-start | bytes 10616836
  7.2 38.5 %all-gather.2.cloned.1.call-start = ((), (), s32[]{:S(2)}) async-start(), calls=%async_computation.3 | async-start | bytes 1310720 | tf_op jit(solution)/shard_map/all_gather | solution.py:49
  10.7 8.5 %collective-permute-start.1 = (bf16[1,2,1,128,128]{3,4,2,1,0:T(8,128)(2,1)}, bf16[1,2,1,128,128]{3,4,2,1,0:T(8,128)(2,1)}, u32[]{:S(2)}, u32[]{:S(2)}) collective-permute-start(bf16[1,2,1,128,128]{3,4,2,1,0:T(8,128)(2,1)} %get-tuple-element.7), channel_id=1, source_target_pairs={{2,0},{4,2},{6,4},{3,1},{5,3},{7,5},{10,8},{12,10},{14,12},{11,9},... | collective-permute-start | bytes 196616 | tf_op jit(solution)/shard_map/ppermute | solution.py:17
  12.0 7.8 %collective-permute-start = (bf16[1,2,1,128,128]{3,4,2,1,0:T(8,128)(2,1)}, bf16[1,2,1,128,128]{3,4,2,1,0:T(8,128)(2,1)}, u32[]{:S(2)}, u32[]{:S(2)}) collective-permute-start(bf16[1,2,1,128,128]{3,4,2,1,0:T(8,128)(2,1)} %get-tuple-element.6), channel_id=1, source_target_pairs={{0,2},{2,4},{4,6},{1,3},{3,5},{5,7},{8,10},{10,12},{12,14},{9,11},... | collective-permute-start | bytes 196616 | tf_op jit(solution)/shard_map/ppermute | solution.py:15
  18.2 53.4 %reduce-scatter.5.cloned.1.call-start = ((), (), s32[]{:S(2)}) async-start(), calls=%async_computation.4 | async-start | bytes 10616832 | tf_op jit(solution)/shard_map/reduce_scatter | solution.py:59
  18.2 3.8 %copy-start.1 = (bf16[1,2,4,128,128]{3,4,2,1,0:T(8,128)(2,1)S(1)}, bf16[1,2,4,128,128]{3,4,2,1,0:T(8,128)(2,1)}, u32[]{:S(2)}) copy-start(bf16[1,2,4,128,128]{3,4,2,1,0:T(8,128)(2,1)} %copy.15) | copy-start | bytes 786436
  24.4 2.9 %copy-start.2 = (bf16[1,2,4,3456,128]{3,4,2,1,0:T(8,128)(2,1)}, bf16[1,2,4,3456,128]{3,4,2,1,0:T(8,128)(2,1)S(1)}, u32[]{:S(2)}) copy-start(bf16[1,2,4,3456,128]{3,4,2,1,0:T(8,128)(2,1)S(1)} %slice_dynamic-update-slice_fusion) | copy-start | bytes 21233668
  56.0 55.9 %reduce-scatter.3.cloned.1.call-start = ((), (), s32[]{:S(2)}) async-start(), calls=%async_computation.2 | async-start | bytes 2621440 | tf_op jit(solution)/shard_map/reduce_scatter | solution.py:66
  63.7 184.3 %all-reduce.3.cloned.1.call-start = ((), (), s32[]{:S(2)}) async-start(), calls=%async_computation.5 | async-start | bytes 7077888 | tf_op jit(solution)/shard_map/psum | solution.py:60
Sparse Core Ops, SparseCore 0:
  18.3 27.2 all-gather.1
  56.2 15.4 reduce-scatter.4
  75.5 36.4 reduce-scatter.2
  114.2 133.7 all-reduce.2
where the time goes:
time: 260 us; the launch traced here: 259 us
  waiting for transfers between devices  187 us (72%)
  local copies, waits for them, and re-layouts  26.3 us (10%)
  matrix products  14.2 us (5%)
  between operations  14 us (5%)
  other arithmetic  9.39 us (4%)
  starting transfers between devices  7.63 us (3%)
    psum x1, waiting for transfers between devices, on_device(): summed = lax.psum(clip_summed, 'space')  132 us
    reduce_scatter x1, waiting for transfers between devices, on_device(): lax.psum_scatter(partial_value, 'chan', scatter_dimension=3, tiled=True)  38.5 us
    dot_general x2, local copies, waits for them, and re-layouts, on_device(): jnp.einsum('cthkw,cthiw->ki', stacked, activated, preferred_element_type=...  14 us
    unnamed x33, local copies, waits for them, and re-layouts  10.7 us
    all_gather x1, waiting for transfers between devices, on_device(): gathered = lax.all_gather(inputs, 'chan', axis=3, tiled=True)  8.09 us
    reduce_scatter x1, waiting for transfers between devices, on_device(): lax.psum_scatter(local_weight, 'rep', scatter_dimension=3, tiled=True)  7.92 us
    dot_general x1, matrix products, on_device(): jnp.einsum('cthkw,ki->cthiw', stacked, flat_kernel, preferred_element_typ...  7.54 us
    dot_general x1, matrix products, on_device(): jnp.einsum('cthkw,cthiw->ki', stacked, activated, preferred_element_type=...  6.64 us
  transfers between devices with their start and end apart: 6, of which 5 were waited for; matrix products, arithmetic and copies ran while one was open for 11% of the time, Pallas kernels for 0%

commit v1 on v0

--- a/solution.py
+++ b/solution.py
@@ -2,6 +2,25 @@
 import jax.numpy as jnp
 from jax import lax
 from jax.sharding import PartitionSpec as P
+
+
+def ring_gather(shard, axis, dim):
+    size, mine, rows = (lax.axis_size(axis), lax.axis_index(axis), shard.shape[dim])
+    right = [(i, (i + 1) % size) for i in range(size)]
+    behind = [(i, (i - 1) % size) for i in range(size)]
+    out = jnp.zeros((*shard.shape[:dim], size * rows, *shard.shape[dim + 1 :]), shard.dtype)
+    out = lax.dynamic_update_slice_in_dim(out, shard, mine * rows, axis=dim)
+    from_left = from_right = shard
+    half = size // 2
+    for turn in range(1, half + 1):
+        from_left = lax.ppermute(from_left, axis, right)
+        out = lax.dynamic_update_slice_in_dim(out, from_left, (mine - turn) % size * rows, axis=dim)
+        if turn < size - half:
+            from_right = lax.ppermute(from_right, axis, behind)
+            out = lax.dynamic_update_slice_in_dim(
+                out, from_right, (mine + turn) % size * rows, axis=dim
+            )
+    return out
 
 
 def with_halo(cells, sides, width):
@@ -46,7 +65,7 @@
 def on_device(inputs, grad_out, weight):
     clip_count, frame_count, row_count, in_part, col_count = inputs.shape
     out_part = grad_out.shape[3]
-    gathered = lax.all_gather(inputs, "chan", axis=3, tiled=True)
+    gathered = ring_gather(inputs, "chan", 3)
     activated = jax.nn.silu(gathered.astype(jnp.float32)).astype(jnp.bfloat16)
     in_width = activated.shape[3]
     grad_rim = with_halo(grad_out, (("space", 2),), 1)

time: 260 us -> 281 us (1.081)
  local copies, waits for them, and re-layouts: 26.3 us -> 47.6 us
  waiting for transfers between devices: 187 us -> 182 us
  starting transfers between devices: 7.63 us -> 11.6 us
    unnamed x33 -> x31, local copies, waits for them, and re-layouts: 10.7 us -> 24.3 us
    all_gather x1 -> x0, waiting for transfers between devices: 8.09 us -> none  [on_device(): gathered = lax.all_gather(inputs, 'chan', axis=3, tiled=True)]
    dynamic_update_slice x0 -> x4, local copies, waits for them, and re-layouts: none -> 5.88 us  [the longest x2 2.48 us: ring_gather(): lax.dynamic_update_slice_in_dim(out, from_left, (mine - turn) % size * ro...]
    ppermute x0 -> x3, starting transfers between devices: none -> 5.02 us  [the longest x2 3.99 us: ring_gather(): from_left = lax.ppermute(from_left, axis, right)]
    ppermute x0 -> x3, waiting for transfers between devices: none -> 3.88 us  [the longest x2 3.88 us: ring_gather(): from_left = lax.ppermute(from_left, axis, right)]
  transfers between devices with their start and end apart: 6 -> 8, of which waited for: 5 -> 4; matrix products, arithmetic and copies ran while one was open for 11% -> 20% of each run, Pallas kernels for 0% -> 0%
where the time goes in v1:
time: 281 us; the launch traced here: 280 us
  waiting for transfers between devices  182 us (65%)
  local copies, waits for them, and re-layouts  47.6 us (17%)
  matrix products  14.2 us (5%)
  between operations  13.8 us (5%)
  starting transfers between devices  11.6 us (4%)
  other arithmetic  10.9 us (4%)
    psum x1, waiting for transfers between devices, on_device(): summed = lax.psum(clip_summed, 'space')  132 us
    reduce_scatter x1, waiting for transfers between devices, on_device(): lax.psum_scatter(partial_value, 'chan', scatter_dimension=3, tiled=True)  38.5 us
    unnamed x31, local copies, waits for them, and re-layouts  24.3 us
    dot_general x2, local copies, waits for them, and re-layouts, on_device(): jnp.einsum('cthkw,cthiw->ki', stacked, activated, preferred_element_type=...  14.1 us
    dot_general x1, matrix products, on_device(): jnp.einsum('cthkw,ki->cthiw', stacked, flat_kernel, preferred_element_typ...  7.54 us
    reduce_scatter x1, waiting for transfers between devices, on_device(): lax.psum_scatter(local_weight, 'rep', scatter_dimension=3, tiled=True)  7.36 us
    dot_general x1, matrix products, on_device(): jnp.einsum('cthkw,cthiw->ki', stacked, activated, preferred_element_type=...  6.64 us
  transfers between devices with their start and end apart: 8, of which 4 were waited for; matrix products, arithmetic and copies ran while one was open for 20% of the time, Pallas kernels for 0%

profile of v1, /device:TPU:0, one launch (start us, length us, event | category | flops | bytes accessed | tf_op | source)
XLA Modules:
  0.0 280.3 jit_solution(15691982863946229920)
XLA Ops:
  7.2 3.0 %collective-permute-start.2 = (bf16[1,2,4,128,128]{4,3,2,1,0:T(8,128)(2,1)}, bf16[1,2,4,128,128]{4,3,2,1,0:T(8,128)(2,1)}, u32[]{:S(2)}, u32[]{:S(2)}) collective-permute-start(bf16[1,2,4,128,128]{4,3,2,1,0:T(8,128)(2,1)} %param.3), channel_id=1, source_target_pairs={{0,8},{8,16},{16,24},{24,0},{1,9},{9,17},{17,25},{25,1},{2,10},{10... | collective-permute-start | bytes 786440 | tf_op jit(solution)/shard_map/ppermute | solution.py:16
  11.2 1.8 copy.18
  13.0 1.5 fusion.34
  14.6 1.3 collective-permute-start.1
  15.9 5.2 %collective-permute-start = (bf16[1,2,1,128,128]{3,4,2,1,0:T(8,128)(2,1)}, bf16[1,2,1,128,128]{3,4,2,1,0:T(8,128)(2,1)}, u32[]{:S(2)}, u32[]{:S(2)}) collective-permute-start(bf16[1,2,1,128,128]{3,4,2,1,0:T(8,128)(2,1)} %get-tuple-element.6), channel_id=1, source_target_pairs={{0,2},{2,4},{4,6},{1,3},{3,5},{5,7},{8,10},{10,12},{12,14},{9,11},... | collective-permute-start | bytes 196616 | tf_op jit(solution)/shard_map/ppermute | solution.py:34
  27.2 1.1 broadcast_in_dim.3
  28.3 1.7 copy_dynamic-update-slice_fusion.3
  30.8 1.2 fusion.21
  40.0 1.7 fusion.32
  45.7 1.6 fusion.31
  48.0 10.3 %copy.25 = bf16[3456,4,2,128]{3,0,2,1:T(8,128)(2,1)} copy(bf16[3456,4,2,128]{0,3,1,2:T(8,128)(2,1)} %bitcast.32) | data formatting | bytes 14155776 | tf_op jit(solution)/shard_map/cthkw,cthiw->ki/dot_general | solution.py:74
  59.4 1.7 copy_dynamic-update-slice_fusion.2
  61.1 1.7 copy_dynamic-update-slice_fusion.1
  62.8 3.9 %collective-permute-done.4 = bf16[1,2,4,128,128]{4,3,2,1,0:T(8,128)(2,1)S(1)} collective-permute-done((bf16[1,2,4,128,128]{4,3,2,1,0:T(8,128)(2,1)}, bf16[1,2,4,128,128]{4,3,2,1,0:T(8,128)(2,1)S(1)}, u32[]{:S(2)}, u32[]{:S(2)}) %collective-permute-start.4) | collective-permute-done | bytes 262176 | tf_op jit(solution)/shard_map/ppermute | solution.py:16
  67.4 6.6 %fusion = f32[3,3,3,128,512,1,1]{4,3,0,1,2,6,5:T(8,128)S(1)} fusion(bf16[3,3,3,128,4,2,128]{6,3,2,1,0,5,4:T(8,128)(2,1)} %bitcast.33, bf16[1,2,4,512,128]{4,3,1,2,0:T(8,128)(2,1)} %copy_dynamic-update-slice_fusion), kind=kOutput, calls=%fused_computation | convolution fusion | flops 3627024384 | bytes 15204352 | tf_op jit(solution)/shard_map/cthkw,cthiw->ki/dot_general | solution.py:74
  74.1 3.7 %copy.44 = f32[3,3,3,128,512,1,1]{4,3,2,1,0,5,6:T(8,128)} copy(f32[3,3,3,128,512,1,1]{4,3,0,1,2,6,5:T(8,128)S(1)} %fusion) | data formatting | bytes 14155776 | tf_op jit(solution)/shard_map/cthkw,cthiw->ki/dot_general | solution.py:74
  77.9 7.5 %fusion.13 = f32[1,2,4,512,128]{3,4,2,1,0:T(8,128)} fusion(bf16[3456,512,1,1]{1,0,3,2:T(8,128)(2,1)S(1)} %bitcast.30, bf16[1,2,4,3456,128]{3,4,2,1,0:T(8,128)(2,1)} %slice_dynamic-update-slice_fusion), kind=kOutput, calls=%fused_computation.20 | convolution fusion | flops 3623878656 | bytes 12713984 | tf_op jit(solution)/shard_map/cthkw,ki->cthiw/dot_general | solution.py:82
  85.5 7.4 %reduce-scatter.5.cloned.1.call-done = f32[3,3,3,64,512]{4,3,2,1,0:T(8,128)} async-done(((f32[3,3,3,128,512]{4,3,2,1,0:T(8,128)}), f32[3,3,3,64,512]{4,3,2,1,0:T(8,128)}) %reduce-scatter.5.cloned.1.call-update) | async-done | bytes 3538960 | tf_op jit(solution)/shard_map/reduce_scatter | solution.py:78
  92.9 1.8 copy.24
  94.7 38.5 %reduce-scatter.3.cloned.1.call-done = f32[1,2,4,128,128]{3,4,2,1,0:T(8,128)} async-done(((f32[1,2,4,512,128]{3,4,2,1,0:T(8,128)}), f32[1,2,4,128,128]{3,4,2,1,0:T(8,128)}) %reduce-scatter.3.cloned.1.call-update) | async-done | bytes 524304 | tf_op jit(solution)/shard_map/reduce_scatter | solution.py:85
  133.1 2.0 fusion.30
  135.1 1.8 copy.31
  136.9 132.4 %all-reduce.3.cloned.1.call-done = f32[3,3,3,64,512]{4,3,2,1,0:T(8,128)} async-done(((f32[3,3,3,64,512]{4,3,2,1,0:T(8,128)}), f32[3,3,3,64,512]{4,3,2,1,0:T(8,128)}) %all-reduce.3.cloned.1.call-update) | async-done | bytes 3538960 | tf_op jit(solution)/shard_map/psum | solution.py:79
  269.3 4.4 %broadcast_multiply_fusion = f32[3,3,3,64,512]{4,3,2,1,0:T(8,128)} fusion(f32[3,3,3,64,512]{4,3,2,1,0:T(8,128)} %all-reduce.3.cloned.1.call-done), kind=kLoop, calls=%fused_computation.13 | loop fusion | flops 884736 | bytes 7077888 | tf_op jit(solution)/shard_map/mul | solution.py:80
  (42 shorter events, 22.6 us)
Async XLA Ops:
  7.2 70.7 %copy-start = (bf16[3,3,3,128,512]{4,3,2,1,0:T(8,128)(2,1)S(1)}, bf16[3,3,3,128,512]{4,3,2,1,0:T(8,128)(2,1)}, u32[]{:S(2)}) copy-start(bf16[3,3,3,128,512]{4,3,2,1,0:T(8,128)(2,1)} %param.5) | copy-start | bytes 10616836
  7.2 85.7 %reduce-scatter.5.cloned.1.call-start = ((), (), s32[]{:S(2)}) async-start(), calls=%async_computation.3 | async-start | bytes 10616832 | tf_op jit(solution)/shard_map/reduce_scatter | solution.py:78
  7.2 51.1 %collective-permute-start.2 = (bf16[1,2,4,128,128]{4,3,2,1,0:T(8,128)(2,1)}, bf16[1,2,4,128,128]{4,3,2,1,0:T(8,128)(2,1)}, u32[]{:S(2)}, u32[]{:S(2)}) collective-permute-start(bf16[1,2,4,128,128]{4,3,2,1,0:T(8,128)(2,1)} %param.3), channel_id=1, source_target_pairs={{0,8},{8,16},{16,24},{24,0},{1,9},{9,17},{17,25},{25,1},{2,10},{10... | collective-permute-start | bytes 786440 | tf_op jit(solution)/shard_map/ppermute | solution.py:16
  10.2 50.9 %collective-permute-start.3 = (bf16[1,2,4,128,128]{4,3,2,1,0:T(8,128)(2,1)}, bf16[1,2,4,128,128]{4,3,2,1,0:T(8,128)(2,1)}, u32[]{:S(2)}, u32[]{:S(2)}) collective-permute-start(bf16[1,2,4,128,128]{4,3,2,1,0:T(8,128)(2,1)} %param.3), channel_id=1, source_target_pairs={{0,24},{8,0},{16,8},{24,16},{1,25},{9,1},{17,9},{25,17},{2,26},{10... | collective-permute-start | bytes 786440 | tf_op jit(solution)/shard_map/ppermute | solution.py:19
  14.6 16.3 %collective-permute-start.1 = (bf16[1,2,1,128,128]{3,4,2,1,0:T(8,128)(2,1)}, bf16[1,2,1,128,128]{3,4,2,1,0:T(8,128)(2,1)}, u32[]{:S(2)}, u32[]{:S(2)}) collective-permute-start(bf16[1,2,1,128,128]{3,4,2,1,0:T(8,128)(2,1)} %get-tuple-element.7), channel_id=1, source_target_pairs={{2,0},{4,2},{6,4},{3,1},{5,3},{7,5},{10,8},{12,10},{14,12},{11,9},... | collective-permute-start | bytes 196616 | tf_op jit(solution)/shard_map/ppermute | solution.py:36
  15.9 15.0 %collective-permute-start = (bf16[1,2,1,128,128]{3,4,2,1,0:T(8,128)(2,1)}, bf16[1,2,1,128,128]{3,4,2,1,0:T(8,128)(2,1)}, u32[]{:S(2)}, u32[]{:S(2)}) collective-permute-start(bf16[1,2,1,128,128]{3,4,2,1,0:T(8,128)(2,1)} %get-tuple-element.6), channel_id=1, source_target_pairs={{0,2},{2,4},{4,6},{1,3},{3,5},{5,7},{8,10},{10,12},{12,14},{9,11},... | collective-permute-start | bytes 196616 | tf_op jit(solution)/shard_map/ppermute | solution.py:34
  30.0 13.3 %copy-start.1 = (bf16[1,2,4,128,128]{3,4,2,1,0:T(8,128)(2,1)S(1)}, bf16[1,2,4,128,128]{3,4,2,1,0:T(8,128)(2,1)}, u32[]{:S(2)}) copy-start(bf16[1,2,4,128,128]{3,4,2,1,0:T(8,128)(2,1)} %copy.18) | copy-start | bytes 786436
  58.4 8.3 %collective-permute-start.4 = (bf16[1,2,4,128,128]{4,3,2,1,0:T(8,128)(2,1)}, bf16[1,2,4,128,128]{4,3,2,1,0:T(8,128)(2,1)S(1)}, u32[]{:S(2)}, u32[]{:S(2)}) collective-permute-start(bf16[1,2,4,128,128]{4,3,2,1,0:T(8,128)(2,1)} %collective-permute-done.2), channel_id=1, source_target_pairs={{0,8},{8,16},{16,24},{24,0},{1,9},{9,17},{17,25},{25,1},{2,10},{10... | collective-permute-start | bytes 786440 | tf_op jit(solution)/shard_map/ppermute | solution.py:16
  77.8 55.3 %reduce-scatter.3.cloned.1.call-start = ((), (), s32[]{:S(2)}) async-start(), calls=%async_computation.2 | async-start | bytes 2621440 | tf_op jit(solution)/shard_map/reduce_scatter | solution.py:85
  85.5 183.9 %all-reduce.3.cloned.1.call-start = ((), (), s32[]{:S(2)}) async-start(), calls=%async_computation.4 | async-start | bytes 7077888 | tf_op jit(solution)/shard_map/psum | solution.py:79
Sparse Core Ops, SparseCore 0:
  77.9 14.8 reduce-scatter.4
  96.7 36.4 reduce-scatter.2
  135.5 133.7 all-reduce.2
